TPU v7x, 32 devices: a whole 2x2x4 slice. The times are simulated.
32 devices in a mesh: grp: 4 (over y, x), tp: 4 (over z), seq: 2 (over core).
Axes of the slice: x: 2, y: 2, z: 4, core: 2. Of those that a mesh axis runs over, the one named last changes fastest.
Arguments:
- grads: bfloat16 [8, 4096, 8192], P(('grp', 'seq'), 'tp'), may hold values from -6 to 6
- master: float32 [4096, 8192], P('tp', 'grp'), may hold values from -0.09375 to 0.09375
- moment: float32 [4096, 8192], P('tp', 'grp'), may hold values from -3 to 3
- second: float32 [4096, 8192], P('tp', 'grp'), may hold values from 0.0001 to 1
- queries: bfloat16 [4096, 4096], P(('grp', 'seq'), 'tp'), may hold values from -7 to 7
- keys: bfloat16 [4096, 512], P(('grp', 'seq')), may hold values from -6 to 6
- values: bfloat16 [4096, 512], P(('grp', 'seq')), may hold values from -6 to 6
- resid: bfloat16 [4096, 8192], P(('grp', 'seq'), 'tp'), may hold values from -6 to 6
- segs: int32 [4096], replicated, may hold values from 0 to 15, never falling along the last dimension, each value on 1 to 512 neighbouring positions
Outputs:
- master_new: float32 [4096, 8192], P('tp', 'grp')
- moment_new: float32 [4096, 8192], P('tp', 'grp')
- second_new: float32 [4096, 8192], P('tp', 'grp')
- layer_out: bfloat16 [4096, 8192], P(('grp', 'seq'), 'tp')
Inputs may be any that keep to these rules, and one draw needn't show every extreme that they name: `segs`: numbered from 0 in order of position and never falling; each trajectory is a run of 1 to 512 positions.
All inputs are finite; a program needn't handle non-finite values.
Results may differ from a plain program's by a relative error of at most 0.0085.
Values may be sent and summed in bfloat16 or wider, within the bound.
A program may use at most 192 MiB of HBM per device.

v0:
```python
import jax
import jax.numpy as jnp
from jax import lax
from jax.sharding import PartitionSpec as P

HD = 128
HQ = 32
KVH = 4


beta_one = 0.9
beta_two = 0.95
learn_rate = 0.001
decay_rate = 0.1
adam_eps = 1e-08


def from_behind(x, axis, by):
    count = lax.axis_size(axis)
    pairs = [(i, i + by) for i in range(count) if 0 <= i + by < count]
    return lax.ppermute(x, axis, pairs)


def body(grads, master, moment, second, queries, keys, values, resid, segs):
    partial_sum = lax.psum_scatter(grads[0], "grp", scatter_dimension=1, tiled=True).astype(
        jnp.float32
    )
    summed = lax.psum(partial_sum.astype(jnp.bfloat16), "seq").astype(jnp.float32)
    gradient = summed / (lax.axis_size("grp") * lax.axis_size("seq"))
    moment_new = beta_one * moment + (1.0 - beta_one) * gradient
    second_new = beta_two * second + (1.0 - beta_two) * gradient * gradient
    first_hat = moment_new / (1.0 - beta_one**10)
    second_hat = second_new / (1.0 - beta_two**10)
    master_new = master - learn_rate * (
        first_hat / (jnp.sqrt(second_hat) + adam_eps) + decay_rate * master
    )
    weight_block = master_new.astype(jnp.bfloat16)
    tok_rows = queries.shape[0]
    heads_here = queries.shape[1] // HD
    key_head = lax.axis_index("tp") * heads_here // (HQ // KVH)
    own_keys = lax.dynamic_slice_in_dim(keys, key_head * HD, HD, 1)
    own_values = lax.dynamic_slice_in_dim(values, key_head * HD, HD, 1)
    prior_k, prior_v = from_behind((own_keys, own_values), ("grp", "seq"), 1)
    all_keys = jnp.concatenate([prior_k, own_keys], axis=0)
    all_values = jnp.concatenate([prior_v, own_values], axis=0)
    start = lax.axis_index(("grp", "seq")) * tok_rows
    seg_here = lax.dynamic_slice_in_dim(segs, start, tok_rows, 0)
    seg_prior = lax.dynamic_slice_in_dim(segs, jnp.maximum(start - tok_rows, 0), tok_rows, 0)
    key_segs = jnp.concatenate([seg_prior, seg_here], axis=0)
    query_pos = start + jnp.arange(tok_rows, dtype=jnp.int32)
    key_pos = start - tok_rows + jnp.arange(2 * tok_rows, dtype=jnp.int32)
    visible = (
        (key_pos[None, :] >= 0)
        & (key_pos[None, :] <= query_pos[:, None])
        & (key_segs[None, :] == seg_here[:, None])
    )
    query_heads = queries.reshape(tok_rows, heads_here, HD)
    scores = jnp.einsum(
        "qhd,kd->hqk", query_heads, all_keys, preferred_element_type=jnp.float32
    ) * (1.0 / HD**0.5)
    masked = jnp.where(visible[None], scores, -1e30)
    largest = jnp.max(masked, axis=2, keepdims=True)
    expo = jnp.where(visible[None], jnp.exp(masked - largest), 0.0)
    probs = (expo / jnp.sum(expo, axis=2, keepdims=True)).astype(jnp.bfloat16)
    heads_out = jnp.einsum("hqk,kd->qhd", probs, all_values, preferred_element_type=jnp.float32)
    attn = heads_out.astype(jnp.bfloat16).reshape(tok_rows, heads_here * HD)
    partial_out = jnp.dot(
        attn,
        lax.all_gather(weight_block, "grp", axis=1, tiled=True),
        preferred_element_type=jnp.float32,
    )
    mixed = lax.psum_scatter(
        partial_out.astype(jnp.bfloat16), "tp", scatter_dimension=1, tiled=True
    ).astype(jnp.float32)
    layer_out = (resid.astype(jnp.float32) + mixed).astype(jnp.bfloat16)
    return (master_new, moment_new, second_new, layer_out)


def solution(mesh):
    placed = (
        P(("grp", "seq"), "tp", None),
        P("tp", "grp"),
        P("tp", "grp"),
        P("tp", "grp"),
        P(("grp", "seq"), "tp"),
        P(("grp", "seq"), None),
        P(("grp", "seq"), None),
        P(("grp", "seq"), "tp"),
        P(),
    )
    return jax.shard_map(
        body,
        mesh=mesh,
        in_specs=placed,
        out_specs=(P("tp", "grp"), P("tp", "grp"), P("tp", "grp"), P(("grp", "seq"), "tp")),
        check_vma=False,
    )
```

profile of v0, /device:TPU:0, one launch (start us, length us, event | category | flops | bytes accessed | tf_op | source)
XLA Modules:
  0.0 551.7 jit_solution(7033099441758645557)
XLA Ops:
  7.2 0.0 reduce-scatter.3.cloned.1.call-start
  7.2 0.7 reduce-scatter.3.cloned.1.call-update
  7.9 0.0 all-reduce.2.cloned.1.call-start
  8.0 159.6 %reduce-scatter.3.cloned.1.call-done = bf16[1024,2048]{1,0:T(8,128)(2,1)} async-done(((bf16[1024,8192]{1,0:T(8,128)(2,1)}), bf16[1024,2048]{1,0:T(8,128)(2,1)}) %reduce-scatter.3.cloned.1.call-update) | async-done | bytes 4194320 | tf_op jit(solution)/shard_map/reduce_scatter | solution.py:25
  167.5 0.0 all-reduce.2.cloned.1.call-update
  167.6 0.0 all-gather.2.cloned.1.call-start
  167.6 30.5 %all-reduce.2.cloned.1.call-done = bf16[1024,2048]{1,0:T(8,128)(2,1)} async-done(((bf16[1024,2048]{1,0:T(8,128)(2,1)}), bf16[1024,2048]{1,0:T(8,128)(2,1)}) %all-reduce.2.cloned.1.call-update) | async-done | bytes 4194320 | tf_op jit(solution)/shard_map/psum | solution.py:28
  198.1 22.9 %fusion.21 = (bf16[1024,2048]{1,0:T(8,128)(2,1)}, f32[1024,2048]{1,0:T(8,128)}, f32[1024,2048]{1,0:T(8,128)}, f32[1024,2048]{1,0:T(8,128)}) fusion(f32[1024,2048]{1,0:T(8,128)} %param.10, bf16[1024,2048]{1,0:T(8,128)(2,1)} %all-reduce.2.cloned.1.call-done, f32[1024,2048]{1,0:T(8,128)} %param.11, f32[1024,2048]{1,0:T(8,128)} %param.12), kind=kLoop, calls=%fused_computation.39 | loop fusion | flops 37748736 | bytes 58720256 | tf_op jit(solution)/shard_map/convert_element_type | solution.py:37
  221.0 0.0 all-gather.2.cloned.1.call-update
  221.0 0.0 reduce-scatter.5.cloned.1.call-start
  221.1 0.9 constant_dynamic-slice_fusion.1
  222.0 0.1 copy.17
  222.1 2.1 collective-permute-start
  224.3 0.9 constant_dynamic-slice_fusion
  225.2 3.5 collective-permute-start.1
  228.8 0.8 fusion.24
  229.6 0.9 compare_and_fusion
  230.6 9.9 %fusion.10 = f32[1024,512,8]{1,0,2:T(8,128)} fusion(bf16[512,128]{1,0:T(8,128)(2,1)S(1)} %constant_dynamic-slice_fusion, bf16[512,128]{1,0:T(8,128)(2,1)S(1)} %collective-permute-done.1, bf16[512,1024]{1,0:T(8,128)(2,1)S(1)} %copy-done), kind=kOutput, calls=%fused_computation.20 | convolution fusion | flops 1074266112 | bytes 18087936 | tf_op jit(solution)/shard_map/qhd,kd->hqk/dot_general | solution.py:58
  240.5 18.0 %fusion.25 = (f32[8,512]{1,0:T(8,128)S(1)}, f32[8,512,1024]{1,2,0:T(8,128)}) fusion(f32[1024,512,8]{1,0,2:T(8,128)} %fusion.10, pred[512,1024]{0,1:T(8,128)(4,1)S(1)} %compare_and_fusion), kind=kOutput, calls=%fused_computation.41 | output fusion | flops 29361152 | bytes 34095104 | tf_op jit(solution)/shard_map/sub | solution.py:63
  258.5 7.0 %fusion.9 = bf16[128,8,512]{2,0,1:T(8,128)(2,1)S(1)} fusion(f32[8,512,1024]{1,2,0:T(8,128)} %get-tuple-element.11, f32[8,512]{1,0:T(8,128)S(1)} %get-tuple-element.10, bf16[512,128]{0,1:T(8,128)(2,1)S(1)} %copy.17, bf16[512,128]{0,1:T(8,128)(2,1)S(1)} %collective-permute-done), kind=kOutput, calls=%fused_computation.19 | convolution fusion | flops 1083179008 | bytes 18104320 | tf_op jit(solution)/shard_map/hqk,kd->qhd/dot_general | solution.py:65
  265.5 114.1 %all-gather.2.cloned.1.call-done = bf16[1024,8192]{1,0:T(8,128)(2,1)} async-done(((bf16[1024,2048]{1,0:T(8,128)(2,1)}), bf16[1024,8192]{1,0:T(8,128)(2,1)}) %all-gather.2.cloned.1.call-update) | async-done | bytes 16777232 | tf_op jit(solution)/shard_map/all_gather | solution.py:69
  379.7 17.0 %convolution_convert_fusion = bf16[512,8192]{1,0:T(8,128)(2,1)} fusion(bf16[512,1024]{0,1:T(8,128)(2,1)S(1)} %bitcast.31, bf16[1024,8192]{1,0:T(8,128)(2,1)} %all-gather.2.cloned.1.call-done), kind=kOutput, calls=%fused_computation.8 | convolution fusion | flops 8594128896 | bytes 26214400 | tf_op jit(solution)/shard_map/dot_general | solution.py:67
  396.7 144.8 %reduce-scatter.5.cloned.1.call-done = bf16[512,2048]{1,0:T(8,128)(2,1)} async-done(((bf16[512,8192]{1,0:T(8,128)(2,1)}), bf16[512,2048]{1,0:T(8,128)(2,1)}) %reduce-scatter.5.cloned.1.call-update) | async-done | bytes 2097168 | tf_op jit(solution)/shard_map/reduce_scatter | solution.py:72
  541.5 3.7 add_convert_fusion
  (12 shorter events, 0.1 us)
Async XLA Ops:
  7.2 223.4 %copy-start = (bf16[512,1024]{1,0:T(8,128)(2,1)S(1)}, bf16[512,1024]{1,0:T(8,128)(2,1)}, u32[]{:S(2)}) copy-start(bf16[512,1024]{1,0:T(8,128)(2,1)} %param.13) | copy-start | bytes 3145732
  7.2 160.3 %reduce-scatter.3.cloned.1.call-start = ((), (), s32[]{:S(2)}) async-start(), calls=%async_computation.2 | async-start | bytes 20971520 | tf_op jit(solution)/shard_map/reduce_scatter | solution.py:25
  7.9 190.2 %all-reduce.2.cloned.1.call-start = ((), (), s32[]{:S(2)}) async-start(), calls=%async_computation.3 | async-start | bytes 8388608 | tf_op jit(solution)/shard_map/psum | solution.py:28
  167.6 212.1 %all-gather.2.cloned.1.call-start = ((), (), s32[]{:S(2)}) async-start(), calls=%async_computation.4 | async-start | bytes 20971520 | tf_op jit(solution)/shard_map/all_gather | solution.py:69
  221.0 320.5 %reduce-scatter.5.cloned.1.call-start = ((), (), s32[]{:S(2)}) async-start(), calls=%async_computation.5 | async-start | bytes 10485760 | tf_op jit(solution)/shard_map/reduce_scatter | solution.py:72
  222.1 36.3 %collective-permute-start = (bf16[512,128]{0,1:T(8,128)(2,1)S(1)}, bf16[512,128]{0,1:T(8,128)(2,1)S(1)}, u32[]{:S(2)}, u32[]{:S(2)}) collective-permute-start(bf16[512,128]{0,1:T(8,128)(2,1)S(1)} %copy.17), channel_id=1, source_target_pairs={{0,1},{1,8},{8,9},{9,16},{16,17},{17,24},{24,25},{2,3},{3,10},{10,... | collective-permute-start | bytes 393224 | tf_op jit(solution)/shard_map/ppermute | solution.py:21
  225.2 5.4 collective-permute-start.1
  379.6 165.5 %copy-start.1 = (bf16[512,1024]{1,0:T(8,128)(2,1)S(1)}, bf16[512,1024]{1,0:T(8,128)(2,1)}, u32[]{:S(2)}) copy-start(bf16[512,1024]{1,0:T(8,128)(2,1)} %param.13) | copy-start | bytes 3145732
  396.7 144.8 %copy-start.2 = (bf16[512,2048]{1,0:T(8,128)(2,1)S(1)}, bf16[512,2048]{1,0:T(8,128)(2,1)}, u32[]{:S(2)}) copy-start(bf16[512,2048]{1,0:T(8,128)(2,1)} %param.16) | copy-start | bytes 6291460
Sparse Core Ops, SparseCore 0:
  11.1 156.4 reduce-scatter.2
  170.0 28.0 all-reduce.1
  221.1 158.4 all-gather.1
  396.8 144.6 reduce-scatter.4
where the time goes:
time: 552 us
  waiting for transfers between devices  450 us (82%)
  other arithmetic  45.5 us (8%)
  matrix products  33.9 us (6%)
  between operations  13.9 us (3%)
  starting transfers between devices  5.83 us (1%)
    reduce_scatter x1, waiting for transfers between devices, body(): lax.psum_scatter(grads[0], 'grp', scatter_dimension=1, tiled=True)  160 us
    reduce_scatter x1, waiting for transfers between devices, body(): lax.psum_scatter(partial_out.astype(jnp.bfloat16), 'tp', scatter_dimensio...  145 us
    all_gather x1, waiting for transfers between devices, body(): lax.all_gather(weight_block, 'grp', axis=1, tiled=True)  114 us
    psum x1, waiting for transfers between devices, body(): lax.psum(partial_sum.astype(jnp.bfloat16), 'seq').astype(jnp.float32)  30.5 us
    convert_element_type x1, other arithmetic, body(): weight_block = master_new.astype(jnp.bfloat16)  22.9 us
    sub x1, other arithmetic, body(): expo = jnp.where(visible[None], jnp.exp(masked - largest), 0.0)  18 us
    dot_general x1, matrix products, body(): jnp.dot(attn, lax.all_gather(weight_block, 'grp', axis=1, tiled=True), pr...  17 us
  transfers between devices with their start and end apart: 6, of which 4 were waited for; matrix products, arithmetic and copies ran while one was open for 7% of the time, Pallas kernels for 0%

commit v1 on v0

--- a/solution.py
+++ b/solution.py
@@ -1,6 +1,10 @@
+import functools
+
 import jax
 import jax.numpy as jnp
 from jax import lax
+from jax.experimental import pallas as pl
+from jax.experimental.pallas import tpu as pltpu
 from jax.sharding import PartitionSpec as P
 
 HD = 128
@@ -76,6 +80,398 @@
     return (master_new, moment_new, second_new, layer_out)
 
 
+WIDE = 128
+
+
+def fused_kernel(
+    grads, master, moment, second, queries, keys, values, segs,
+    gsum, mixed,
+    own, recv1, recv2, recv3, wg, rz, attn, qbuf, kbuf, vbuf, adam, segk,
+    own_sem, pair_s, pair_r, st1_s, st1_r, st2_s, st2_r, st3_s, st3_r, st3_l,
+    ag_s, ag_r, z_s, z_r, fin_s, fin_r, fin_l, adam_sem, in_sem, kv_s, kv_r, at_s, at_r,
+):
+    rows = master.shape[0]
+    blk = master.shape[1]
+    half = blk // 2
+    chunks = half // WIDE
+    n_grp = lax.axis_size("grp")
+    n_tp = lax.axis_size("tp")
+    tok = queries.shape[0]
+    f32 = jnp.float32
+    bf16 = jnp.bfloat16
+    g = lax.axis_index("grp")
+    t = lax.axis_index("tp")
+    s = lax.axis_index("seq")
+    x = lax.rem(g, 2)
+    across_x = g + 1 - 2 * x
+    across_y = g + 2 - 4 * lax.div(g, 2)
+    one = across_x * (1 - s) + across_y * s
+    two = across_y * (1 - s) + across_x * s
+    diag = 3 - g
+    up = lax.rem(t + 1, n_tp)
+    down = lax.rem(t + n_tp - 1, n_tp)
+    spot = 2 * g + s
+    n_spot = 2 * n_grp
+    after = lax.rem(spot + 1, n_spot)
+    before = lax.rem(spot + n_spot - 1, n_spot)
+
+    def dev(gg, tt, ss):
+        return {"grp": gg, "tp": tt, "seq": ss}
+
+    peer = dev(g, t, 1 - s)
+    first = dev(one, t, s)
+    last = dev(two, t, s)
+    above = dev(g, up, s)
+    below = dev(g, down, s)
+    nxt = dev(lax.div(after, 2), t, lax.rem(after, 2))
+    prv = dev(lax.div(before, 2), t, lax.rem(before, 2))
+
+    def remote(src, dst, a, b, to):
+        return pltpu.make_async_remote_copy(
+            src_ref=src, dst_ref=dst, send_sem=a, recv_sem=b,
+            device_id=to, device_id_type=pl.DeviceIdType.MESH,
+        )
+
+    def cols(start):
+        return pl.ds(pl.multiple_of(start, WIDE), WIDE)
+
+    def take(j, b):
+        return pltpu.make_async_copy(
+            grads.at[0, :, cols(b * blk + s * half + j * WIDE)], own.at[j, b], own_sem.at[j, b]
+        )
+
+    def pair(j, b):
+        return remote(
+            grads.at[0, :, cols(b * blk + (1 - s) * half + j * WIDE)],
+            recv1.at[j, b], pair_s.at[j, b], pair_r.at[j, b], peer,
+        )
+
+    def state(j, k):
+        ref = (master, moment, second)[k]
+        slot = lax.rem(j, 3)
+        return pltpu.make_async_copy(
+            ref.at[:, cols(s * half + j * WIDE)], adam.at[slot, k], adam_sem.at[slot, k]
+        )
+
+    def hop_one(j, k):
+        b = (one, diag)[k]
+        return remote(own.at[j, b], recv2.at[j, k], st1_s.at[j, k], st1_r.at[j, k], first)
+
+    def hop_two(j):
+        return remote(own.at[j, two], recv3.at[j], st2_s.at[j], st2_r.at[j], last)
+
+    def share(j):
+        where = cols(s * half + j * WIDE)
+        return remote(own.at[j, g], gsum.at[:, where], st3_s.at[j], st3_r.at[j], peer)
+
+    def keep(j):
+        where = cols(s * half + j * WIDE)
+        return pltpu.make_async_copy(own.at[j, g], gsum.at[:, where], st3_l.at[j])
+
+    def spread(j, k):
+        b = (g, g, two)[k]
+        to = (last, first, first)[k]
+        part = wg.at[j, :, cols(b * WIDE)]
+        return remote(part, part, ag_s.at[j, k], ag_r.at[j, k], to)
+
+    def ring(j, d, r):
+        b = lax.rem(t + 2 * n_tp - 1 - r, n_tp) if d == 0 else lax.rem(t + 1 + r, n_tp)
+        return remote(
+            recv1.at[j, b, pl.ds(d * tok, tok)], rz.at[j, d, r],
+            z_s.at[j, 3 * d + r], z_r.at[j, 3 * d + r], above if d == 0 else below,
+        )
+
+    def final_peer(j):
+        src = recv1.at[j, t, pl.ds(pl.multiple_of((1 - s) * tok, tok), tok)]
+        return remote(src, mixed.at[:, cols(s * half + j * WIDE)], fin_s.at[j], fin_r.at[j], peer)
+
+    def final_own(j):
+        src = recv1.at[j, t, pl.ds(pl.multiple_of(s * tok, tok), tok)]
+        return pltpu.make_async_copy(src, mixed.at[:, cols(s * half + j * WIDE)], fin_l.at[j])
+
+    def fetch(j):
+        for b in range(4):
+            pair(j, b).start()
+            take(j, b).start()
+
+    step = 128
+    q_rows = 128
+    q_blocks = tok // q_rows
+
+    def attn_part(i):
+        part = attn.at[pl.ds(pl.multiple_of(s * tok + i * q_rows, q_rows), q_rows)]
+        return remote(part, part, at_s.at[i], at_r.at[i], peer)
+
+    q_copy = pltpu.make_async_copy(queries, qbuf, in_sem.at[0])
+    k_copy = pltpu.make_async_copy(keys.at[:, cols(t * WIDE)], kbuf.at[pl.ds(tok, tok)], in_sem.at[1])
+    v_copy = pltpu.make_async_copy(values.at[:, cols(t * WIDE)], vbuf.at[pl.ds(tok, tok)], in_sem.at[2])
+    k_send = remote(keys.at[:, cols(t * WIDE)], kbuf.at[pl.ds(0, tok)], kv_s.at[0], kv_r.at[0], nxt)
+    v_send = remote(values.at[:, cols(t * WIDE)], vbuf.at[pl.ds(0, tok)], kv_s.at[1], kv_r.at[1], nxt)
+
+    barrier = pltpu.get_barrier_semaphore()
+    for who in (peer, first, last, above, below, nxt, prv):
+        pl.semaphore_signal(barrier, inc=1, device_id=who, device_id_type=pl.DeviceIdType.MESH)
+    q_copy.start()
+    k_copy.start()
+    v_copy.start()
+    pl.semaphore_wait(barrier, 7)
+    fetch(0)
+    k_send.start()
+    v_send.start()
+    fetch(1)
+    fetch(2)
+    segk[:, pl.ds(0, tok)] = segs[:, pl.ds(pl.multiple_of(before * tok, tok), tok)].astype(f32)
+    segk[:, pl.ds(tok, tok)] = segs[:, pl.ds(pl.multiple_of(spot * tok, tok), tok)].astype(f32)
+
+    def over_rows(count, size, fn):
+        @pl.loop(0, count)
+        def _(i):
+            fn(pl.ds(pl.multiple_of(i * size, size), size))
+
+    def stage_one(j):
+        for b in range(4):
+            take(j, b).wait()
+            pair(j, b).wait_recv()
+        for k in range(2):
+            b = (one, diag)[k]
+
+            def add(r):
+                total = own[j, b, r, :].astype(f32) + recv1[j, b, r, :].astype(f32)
+                own[j, b, r, :] = total.astype(bf16)
+
+            over_rows(rows // step, step, add)
+            hop_one(j, k).start()
+
+    def stage_two(j):
+        hop_one(j, 1).wait_recv()
+
+        def add(r):
+            total = own[j, two, r, :].astype(f32) + recv1[j, two, r, :].astype(f32)
+            own[j, two, r, :] = (total + recv2[j, 1, r, :].astype(f32)).astype(bf16)
+
+        over_rows(rows // step, step, add)
+        hop_two(j).start()
+
+    def stage_three(j):
+        hop_one(j, 0).wait_recv()
+        hop_two(j).wait_recv()
+        for k in range(3):
+            state(j, k).wait()
+        slot = lax.rem(j, 3)
+
+        def add(r):
+            total = own[j, g, r, :].astype(f32) + recv1[j, g, r, :].astype(f32)
+            total = total + recv2[j, 0, r, :].astype(f32) + recv3[j, r, :].astype(f32)
+            own[j, g, r, :] = total.astype(bf16)
+            new = adam_step(
+                total.astype(bf16).astype(f32) / n_spot,
+                adam[slot, 0, r, :], adam[slot, 1, r, :], adam[slot, 2, r, :],
+            )[0]
+            wg[j, r, cols(g * WIDE)] = new.astype(bf16)
+
+        over_rows(rows // 64, 64, add)
+        spread(j, 0).start()
+        spread(j, 1).start()
+        share(j).start()
+        keep(j).start()
+
+    def stage_four(j):
+        spread(j, 0).wait_recv()
+        spread(j, 2).start()
+
+    def attend(i):
+        @pl.when(i == 0)
+        def _():
+            q_copy.wait()
+            k_copy.wait()
+            v_copy.wait()
+            k_send.wait_recv()
+            v_send.wait_recv()
+
+        span = tok + q_rows
+        window = pl.ds(pl.multiple_of(i * q_rows, q_rows), span)
+        q_at = pl.ds(pl.multiple_of(i * q_rows, q_rows), q_rows)
+        out_at = pl.ds(pl.multiple_of(s * tok + i * q_rows, q_rows), q_rows)
+        k_seg = segk[:, window]
+        q_row = segk[:, pl.ds(pl.multiple_of(tok + i * q_rows, q_rows), q_rows)]
+        q_seg = jnp.broadcast_to(q_row, (q_rows, q_rows)).T[:, :1]
+        r_id = lax.broadcasted_iota(jnp.int32, (q_rows, span), 0)
+        c_id = lax.broadcasted_iota(jnp.int32, (q_rows, span), 1)
+        visible = (
+            (c_id - tok <= r_id)
+            & ((spot - 1) * tok + i * q_rows + c_id >= 0)
+            & (k_seg == q_seg)
+        )
+        bias = jnp.where(visible, 0.0, -1e30)
+        k_all = kbuf[window, :]
+        v_all = vbuf[window, :]
+
+        @pl.loop(0, queries.shape[1] // HD)
+        def _(h):
+            head = cols(h * HD)
+            scores = lax.dot_general(
+                qbuf[q_at, head], k_all, (((1,), (1,)), ((), ())), preferred_element_type=f32
+            )
+            scores = scores * (1.0 / HD**0.5) + bias
+            expo = jnp.exp(scores - jnp.max(scores, axis=1, keepdims=True))
+            probs = (expo * (1.0 / jnp.sum(expo, axis=1, keepdims=True))).astype(bf16)
+            out = jnp.dot(probs, v_all, preferred_element_type=f32)
+            attn[out_at, head] = out.astype(bf16)
+
+        attn_part(i).start()
+
+    def stage_five(j):
+        @pl.when(j == 0)
+        def _():
+            for i in range(q_blocks):
+                attn_part(i).wait_recv()
+
+        spread(j, 1).wait_recv()
+        spread(j, 2).wait_recv()
+
+        def mul(r):
+            out = jnp.dot(attn[r, :], wg[j], preferred_element_type=f32).astype(bf16)
+            for b in range(4):
+                recv1[j, b, r, :] = out[:, b * WIDE : (b + 1) * WIDE]
+
+        over_rows(2 * tok // 256, 256, mul)
+        ring(j, 0, 0).start()
+        ring(j, 1, 0).start()
+
+    def stage_ring(j, r):
+        for d in range(2):
+            ring(j, d, r - 1).wait_recv()
+            b = lax.rem(t + 2 * n_tp - 1 - r, n_tp) if d == 0 else lax.rem(t + 1 + r, n_tp)
+
+            def add(at):
+                here = pl.ds(pl.multiple_of(d * tok + at.start, step), step)
+                total = recv1[j, b, here, :].astype(f32) + rz[j, d, r - 1, at, :].astype(f32)
+                recv1[j, b, here, :] = total.astype(bf16)
+
+            over_rows(tok // step, step, add)
+            if r < 3:
+                ring(j, d, r).start()
+        if r == 3:
+            final_peer(j).start()
+            final_own(j).start()
+
+    def when(i, lag, fn):
+        @pl.when((i >= lag) & (i < chunks + lag))
+        def _():
+            fn(i - lag)
+
+    @pl.loop(0, chunks + 8)
+    def _(i):
+        @pl.when(i + 3 < chunks)
+        def _():
+            fetch(i + 3)
+
+        @pl.when(i < chunks)
+        def _():
+            for k in range(3):
+                state(i, k).start()
+            stage_one(i)
+
+        when(i, 1, stage_two)
+        when(i, 2, stage_three)
+        when(i, 3, stage_four)
+
+        @pl.when(i < q_blocks)
+        def _():
+            attend(i)
+
+        when(i, 4, stage_five)
+        when(i, 5, lambda j: stage_ring(j, 1))
+        when(i, 6, lambda j: stage_ring(j, 2))
+        when(i, 7, lambda j: stage_ring(j, 3))
+
+    k_send.wait_send()
+    v_send.wait_send()
+
+    @pl.loop(0, q_blocks)
+    def _(i):
+        attn_part(i).wait_send()
+
+    @pl.loop(0, chunks)
+    def _(j):
+        for b in range(4):
+            pair(j, b).wait_send()
+        for k in range(2):
+            hop_one(j, k).wait_send()
+        hop_two(j).wait_send()
+        share(j).wait()
+        keep(j).wait()
+        for k in range(3):
+            spread(j, k).wait_send()
+        for d in range(2):
+            for r in range(3):
+                ring(j, d, r).wait_send()
+        final_peer(j).wait()
+        final_own(j).wait()
+
+
+def adam_step(gradient, master, moment, second):
+    moment_new = beta_one * moment + (1.0 - beta_one) * gradient
+    second_new = beta_two * second + (1.0 - beta_two) * gradient * gradient
+    first_hat = moment_new / (1.0 - beta_one**10)
+    second_hat = second_new / (1.0 - beta_two**10)
+    master_new = master - learn_rate * (
+        first_hat / (jnp.sqrt(second_hat) + adam_eps) + decay_rate * master
+    )
+    return master_new, moment_new, second_new
+
+
+def fused_body(grads, master, moment, second, queries, keys, values, resid, segs):
+    rows, blk = master.shape
+    tok = queries.shape[0]
+    half = blk // 2
+    chunks = half // WIDE
+    n_grp = lax.axis_size("grp")
+    bf16 = jnp.bfloat16
+    dma = pltpu.SemaphoreType.DMA
+    anywhere = pl.BlockSpec(memory_space=pl.ANY)
+    gsum, mixed = pl.pallas_call(
+        fused_kernel,
+        out_shape=(
+            jax.ShapeDtypeStruct((rows, blk), bf16),
+            jax.ShapeDtypeStruct(resid.shape, bf16),
+        ),
+        in_specs=[anywhere] * 7 + [pl.BlockSpec(memory_space=pltpu.VMEM)],
+        out_specs=(anywhere, anywhere),
+        scratch_shapes=[
+            pltpu.VMEM((chunks, n_grp, rows, WIDE), bf16),
+            pltpu.VMEM((chunks, n_grp, rows, WIDE), bf16),
+            pltpu.VMEM((chunks, 2, rows, WIDE), bf16),
+            pltpu.VMEM((chunks, rows, WIDE), bf16),
+            pltpu.VMEM((chunks, rows, n_grp * WIDE), bf16),
+            pltpu.VMEM((chunks, 2, 3, tok, WIDE), bf16),
+            pltpu.VMEM((2 * tok, queries.shape[1]), bf16),
+            pltpu.VMEM(queries.shape, bf16),
+            pltpu.VMEM((2 * tok, HD), bf16),
+            pltpu.VMEM((2 * tok, HD), bf16),
+            pltpu.VMEM((3, 3, rows, WIDE), jnp.float32),
+            pltpu.VMEM((1, 2 * tok), jnp.float32),
+            dma((chunks, 4)), dma((chunks, 4)), dma((chunks, 4)),
+            dma((chunks, 2)), dma((chunks, 2)),
+            dma((chunks,)), dma((chunks,)),
+            dma((chunks,)), dma((chunks,)), dma((chunks,)),
+            dma((chunks, 3)), dma((chunks, 3)),
+            dma((chunks, 6)), dma((chunks, 6)),
+            dma((chunks,)), dma((chunks,)), dma((chunks,)),
+            dma((3, 3)), dma((3,)), dma((2,)), dma((2,)),
+            dma((tok // 128,)), dma((tok // 128,)),
+        ],
+        compiler_params=pltpu.CompilerParams(
+            collective_id=0, has_side_effects=True, vmem_limit_bytes=62 * 1024 * 1024
+        ),
+        name="step",
+    )(grads, master, moment, second, queries, keys, values, segs.reshape(1, -1))
+    gradient = gsum.astype(jnp.float32) / (n_grp * lax.axis_size("seq"))
+    master_new, moment_new, second_new = adam_step(gradient, master, moment, second)
+    layer_out = (resid.astype(jnp.float32) + mixed.astype(jnp.float32)).astype(bf16)
+    return (master_new, moment_new, second_new, layer_out)
+
+
 def solution(mesh):
     placed = (
         P(("grp", "seq"), "tp", None),
@@ -88,8 +484,10 @@
         P(("grp", "seq"), "tp"),
         P(),
     )
+    sizes = dict(mesh.shape)
+    square = sizes["grp"] == 4 and sizes["tp"] == 4 and sizes["seq"] == 2
     return jax.shard_map(
-        body,
+        fused_body if square else body,
         mesh=mesh,
         in_specs=placed,
         out_specs=(P("tp", "grp"), P("tp", "grp"), P("tp", "grp"), P(("grp", "seq"), "tp")),

time: 552 us -> 243 us (0.44)
  waiting for transfers between devices: 450 us -> 0 us
  Pallas kernels: 0 us -> 217 us
  matrix products: 33.9 us -> 0 us
  other arithmetic: 45.5 us -> 24.6 us
  between operations: 13.9 us -> 0.64 us
  starting transfers between devices: 5.83 us -> 0 us
    reduce_scatter x2 -> x0, waiting for transfers between devices: 304 us -> none  [the longest x1 160 us: body(): lax.psum_scatter(grads[0], 'grp', scatter_dimension=1, tiled=True)]
    pallas_call x0 -> x1, Pallas kernels: none -> 217 us  [fused_body(): pl.pallas_call(fused_kernel, out_shape=(jax.ShapeDtypeStruct((rows, blk),...]
    all_gather x1 -> x0, waiting for transfers between devices: 114 us -> none  [body(): lax.all_gather(weight_block, 'grp', axis=1, tiled=True)]
    dot_general x3 -> x0, matrix products: 33.9 us -> none  [the longest x1 17 us: body(): jnp.dot(attn, lax.all_gather(weight_block, 'grp', axis=1, tiled=True), pr...]
    psum x1 -> x0, waiting for transfers between devices: 30.5 us -> none  [body(): lax.psum(partial_sum.astype(jnp.bfloat16), 'seq').astype(jnp.float32)]
    convert_element_type x2 -> x1, other arithmetic: 26.5 us -> 4.44 us  [fused_body(): (resid.astype(jnp.float32) + mixed.astype(jnp.float32)).astype(bf16)]
    ppermute x2 -> x0, starting transfers between devices: 5.68 us -> none  [from_behind(): return lax.ppermute(x, axis, pairs)]
  transfers between devices with their start and end apart: 6 -> 0, of which waited for: 4 -> 0; matrix products, arithmetic and copies ran while one was open for 7% -> 0% of each run, Pallas kernels for 0% -> 0%
where the time goes in v1:
time: 243 us; the launch traced here: 242 us
  Pallas kernels  217 us (89%)
  other arithmetic  24.6 us (10%)
    pallas_call x1, Pallas kernels, fused_body(): pl.pallas_call(fused_kernel, out_shape=(jax.ShapeDtypeStruct((rows, blk),...  217 us
    sub x1, other arithmetic, adam_step(): master - learn_rate * (first_hat / (jnp.sqrt(second_hat) + adam_eps) + de...  20.2 us

profile of v1, /device:TPU:0, one launch (start us, length us, event | category | flops | bytes accessed | tf_op | source)
XLA Modules:
  0.0 242.5 jit_solution(11444371643482787122)
XLA Ops:
  0.6 217.2 %step.1 = (bf16[1024,2048]{1,0:T(8,128)(2,1)}, bf16[512,2048]{1,0:T(8,128)(2,1)}) custom-call(bf16[1,1024,8192]{2,1,0:T(8,128)(2,1)} %grads.1, f32[1024,2048]{1,0:T(8,128)} %master.1, f32[1024,2048]{1,0:T(8,128)} %moment.1, f32[1024,2048]{1,0:T(8,128)} %second.1, bf16[512,1024]{1,0:T(8,128)(2,1)} %queries.1, bf16[512,512]{1,0:T(8,128)(2,1)} %keys.1, ...), custom_call_target="tpu_custom_call" | custom-call | tf_op jit(solution)/shard_map/step/pallas_call | solution.py:433
  217.8 4.4 %add_convert_fusion = bf16[512,2048]{1,0:T(8,128)(2,1)} fusion(bf16[512,2048]{1,0:T(8,128)(2,1)} %get-tuple-element.7, bf16[512,2048]{1,0:T(8,128)(2,1)} %param.16), kind=kLoop, calls=%fused_computation.7 | loop fusion | flops 4194304 | bytes 6291456 | tf_op jit(solution)/shard_map/convert_element_type | solution.py:471
  222.3 20.2 %multiply_subtract_fusion = (f32[1024,2048]{1,0:T(8,128)}, f32[1024,2048]{1,0:T(8,128)}, f32[1024,2048]{1,0:T(8,128)}) fusion(f32[1024,2048]{1,0:T(8,128)} %master.1, bf16[1024,2048]{1,0:T(8,128)(2,1)} %get-tuple-element.6, f32[1024,2048]{1,0:T(8,128)} %moment.1, f32[1024,2048]{1,0:T(8,128)} %second.1), kind=kLoop, calls=%fused_computation.6 | loop fusion | flops 35651584 | bytes 54525952 | tf_op jit(solution)/shard_map/sub | solution.py:418
